TPU v7x, 512 devices: a whole 4x4x16 slice. The times are simulated.
512 devices in a mesh: expert: 32 (over z, x_lo), fsdp: 16 (over x_hi, y, core).
Axes of the slice: x: 4 (x_hi: 2, x_lo: 2; x = x_hi * 2 + x_lo), y: 4, z: 16, core: 2. Of those that a mesh axis runs over, the one named last changes fastest.
Arguments:
- tokens: bfloat16 [3584, 4096], P(('expert', 'fsdp')), may hold values from -6 to 6
- expert_ids: int32 [3584, 8], P(('expert', 'fsdp')), may hold values from 0 to 31, all different within a row; in each aligned block of 7 rows (0 to 6, 7 to 13, ...) at most 2 rows name the same one
- gate_scores: float32 [3584, 8], P(('expert', 'fsdp')), may hold values from 0.05 to 1
- w_gate: bfloat16 [32, 1536, 4096], P('expert', 'fsdp'), may hold values from -0.09375 to 0.09375
- w_up: bfloat16 [32, 1536, 4096], P('expert', 'fsdp'), may hold values from -0.09375 to 0.09375
- w_down: bfloat16 [32, 1536, 4096], P('expert', None, 'fsdp'), may hold values from -0.15625 to 0.15625
Outputs:
- mixed: bfloat16 [3584, 4096], P(('expert', 'fsdp'))
Inputs may be any that keep to these rules, and one draw needn't show every extreme that they name: `expert_ids`: each token names 8 different experts. Within the 7 tokens of one device (aligned blocks of rows) no expert is named more than 2 times, and in every draw some expert is named exactly 2 times in some block.
All inputs are finite; a program needn't handle non-finite values.
Results may differ from a plain program's by a relative error of at most 0.0057.
Values may be sent and summed in bfloat16 or wider, within the bound.
A program may use at most 64 MiB of HBM per device.

v0:
```python
import jax
import jax.numpy as jnp
from jax import lax
from jax.sharding import PartitionSpec as P


def on_device(tokens, expert_ids, gate_scores, w_gate, w_up, w_down):
    n_expert = lax.axis_size("expert")
    n_fsdp = lax.axis_size("fsdp")
    local_tok, top_k = expert_ids.shape
    per_column = w_gate.shape[0]
    experts = per_column * n_expert
    capacity = min(local_tok, max(2, 3 * local_tok * top_k // (2 * experts)))
    width = tokens.shape[1]
    feature_cols = w_down.shape[2]
    weights = gate_scores / jnp.sum(gate_scores, axis=1, keepdims=True)
    expert_iota = lax.broadcasted_iota(jnp.int32, (1, 1, experts), 2)
    matches = (expert_ids[:, :, None] == expert_iota).astype(jnp.int32)
    chosen = jnp.sum(matches, axis=1, dtype=jnp.int32)
    weight_table = jnp.sum(weights[:, :, None] * matches.astype(jnp.float32), axis=1)
    ranks = jnp.cumsum(chosen, axis=0, dtype=jnp.int32) - chosen
    slot_iota = lax.broadcasted_iota(jnp.int32, (1, 1, capacity), 2)
    slot_mask = jnp.logical_and(ranks[:, :, None] == slot_iota, chosen[:, :, None] > 0)
    select_f32 = jnp.transpose(slot_mask.astype(jnp.float32), (1, 2, 0))
    select_bf = select_f32.astype(jnp.bfloat16)
    combine_table = select_f32 * jnp.transpose(weight_table)[:, None, :]
    outgoing = jnp.einsum("ect,td->ecd", select_bf, tokens, preferred_element_type=jnp.float32)
    outgoing = outgoing.astype(jnp.bfloat16)
    arrived = lax.all_to_all(outgoing, "expert", split_axis=0, concat_axis=0, tiled=True)
    portion = lax.all_gather(arrived[None], "fsdp", axis=0, tiled=True)
    routed = portion.reshape(portion.shape[0], n_expert, per_column, capacity, width)
    gate_act = jnp.einsum("knjcd,jhd->knjch", routed, w_gate, preferred_element_type=jnp.float32)
    up_act = jnp.einsum("knjcd,jhd->knjch", routed, w_up, preferred_element_type=jnp.float32)
    hidden = (jax.nn.silu(gate_act) * up_act).astype(jnp.bfloat16)
    summed = jnp.einsum(
        "fnjch,jhd->fnjcd",
        lax.all_gather(hidden, "fsdp", axis=4, tiled=True),
        w_down,
        preferred_element_type=jnp.float32,
    )
    expert_out = summed.astype(jnp.bfloat16).reshape(
        n_fsdp, n_expert, per_column * capacity, feature_cols
    )
    returned = lax.all_to_all(
        lax.all_to_all(expert_out, "expert", split_axis=1, concat_axis=1, tiled=True),
        "fsdp",
        split_axis=0,
        concat_axis=3,
        tiled=True,
    )
    returned = returned.reshape(experts, capacity, width)
    mixed = jnp.einsum(
        "ect,ecd->td", combine_table, returned.astype(jnp.float32), precision=lax.Precision.HIGHEST
    )
    return mixed.astype(jnp.bfloat16)


def solution(mesh):
    placed = (
        P(("expert", "fsdp"), None),
        P(("expert", "fsdp"), None),
        P(("expert", "fsdp"), None),
        P("expert", "fsdp", None),
        P("expert", "fsdp", None),
        P("expert", None, "fsdp"),
    )
    return jax.shard_map(
        on_device,
        mesh=mesh,
        in_specs=placed,
        out_specs=P(("expert", "fsdp"), None),
        check_vma=False,
    )
```

profile of v0, /device:TPU:1, one launch (start us, length us, event | category | flops | bytes accessed | tf_op | source)
XLA Modules:
  0.0 343.0 jit_solution(12220957122521888835)
XLA Ops:
  6.5 0.0 copy-start
  6.5 0.0 all-gather.6.cloned.1.call-start
  6.5 0.8 convert_reduce_fusion
  7.4 1.2 convolution_convert_fusion
  8.6 0.5 copy.34
  9.2 48.1 %all_to_all.25 = bf16[32,2,4096]{2,1,0:T(2,128)(2,1)S(1)} all-to-all(bf16[32,2,4096]{2,1,0:T(2,128)(2,1)S(1)} %copy.34), channel_id=1, replica_groups=mesh['expert'=32,'fsdp'=16] {'expert'}, dimensions={0} | all-to-all | bytes 1048576 | tf_op jit(solution)/shard_map/all_to_all | solution.py:29
  57.3 1.1 copy.35
  58.4 0.0 all-gather.6.cloned.1.call-update
  58.4 0.0 all-gather.4.cloned.1.call-start
  58.5 82.3 %all-gather.6.cloned.1.call-done = bf16[512,2,4096]{2,0,1:T(8,128)(2,1)} async-done(((bf16[32,2,4096]{2,0,1:T(8,128)(2,1)}), bf16[512,2,4096]{2,0,1:T(8,128)(2,1)}) %all-gather.6.cloned.1.call-update) | async-done | bytes 8388624 | tf_op jit(solution)/shard_map/all_gather | solution.py:30
  140.8 0.0 copy-start.3
  140.8 0.0 copy-start.4
  140.8 6.0 %fusion.10 = f32[16,32,1,2,96]{4,1,3,0,2:T(8,128)S(1)} fusion(bf16[16,32,2,4096]{3,1,0,2:T(8,128)(2,1)} %bitcast.65, bf16[1,96,4096]{2,1,0:T(8,128)(2,1)} %param.9), kind=kOutput, calls=%fused_computation.10 | convolution fusion | flops 805306368 | bytes 9568256 | tf_op jit(solution)/shard_map/knjcd,jhd->knjch/dot_general | solution.py:32
  146.8 0.0 copy-done.3
  146.8 0.1 copy-done.4
  146.9 2.3 fusion.19
  149.3 2.1 copy.38
  151.3 0.0 all-gather.4.cloned.1.call-update
  151.4 103.8 %all-gather.4.cloned.1.call-done = bf16[16,32,1,2,1536]{1,0,3,2,4:T(8,128)(2,1)} async-done(((bf16[16,32,1,2,96]{1,0,3,2,4:T(8,128)(2,1)}), bf16[16,32,1,2,1536]{1,0,3,2,4:T(8,128)(2,1)}) %all-gather.4.cloned.1.call-update) | async-done | bytes 3145744 | tf_op jit(solution)/shard_map/all_gather | solution.py:37
  255.2 13.4 %copy.39 = bf16[16,32,1,2,1536]{4,1,3,0,2:T(8,128)(2,1)} copy(bf16[16,32,1,2,1536]{1,0,3,2,4:T(8,128)(2,1)} %all-gather.4.cloned.1.call-done) | data formatting | bytes 6291456 | tf_op jit(solution)/shard_map/all_gather | solution.py:37
  268.6 0.0 copy-done
  268.6 0.0 copy-start.2
  268.6 0.0 copy-start.1
  268.6 2.9 fusion.7
  271.5 0.5 copy.40
  272.0 44.3 %all_to_all.26 = bf16[16,32,2,256]{3,2,0,1:T(2,128)(2,1)S(1)} all-to-all(bf16[16,32,2,256]{3,2,0,1:T(2,128)(2,1)S(1)} %copy.40), channel_id=1, replica_groups=mesh['expert'=32,'fsdp'=16] {'expert'}, dimensions={1} | all-to-all | bytes 1048576 | tf_op jit(solution)/shard_map/all_to_all | solution.py:45
  316.4 1.3 copy.41
  317.7 5.8 %all-to-all-start.2 = ((bf16[16,32,2,256]{3,2,1,0:T(2,128)(2,1)}), bf16[16,32,2,256]{3,2,1,0:T(2,128)(2,1)S(1)}, u32[]{:S(2)}, u32[]{:S(2)}) async-start(bf16[16,32,2,256]{3,2,1,0:T(2,128)(2,1)} %copy.41), calls=%async_computation.2 | async-start | bytes 1048576 | tf_op jit(solution)/shard_map/all_to_all | solution.py:44
  323.4 0.0 copy-done.2
  323.4 0.1 reduce_sum.28
  323.6 0.1 broadcast_divide_fusion
  323.6 0.0 copy-done.1
  323.6 0.1 fusion.27
  323.7 10.9 %all-to-all-done.2 = bf16[16,32,2,256]{3,2,1,0:T(2,128)(2,1)S(1)} async-done(((bf16[16,32,2,256]{3,2,1,0:T(2,128)(2,1)}), bf16[16,32,2,256]{3,2,1,0:T(2,128)(2,1)S(1)}, u32[]{:S(2)}, u32[]{:S(2)}) %all-to-all-start.2) | async-done | bytes 524320 | tf_op jit(solution)/shard_map/all_to_all | solution.py:44
  334.6 0.3 copy.42
  334.9 0.2 reshape.47
  335.2 1.0 fusion.4
  (3 shorter events, 0.0 us)
Async XLA Ops:
  6.5 262.1 %copy-start = (bf16[1,1536,256]{2,1,0:T(8,128)(2,1)S(1)}, bf16[1,1536,256]{2,1,0:T(8,128)(2,1)}, u32[]{:S(2)}) copy-start(bf16[1,1536,256]{2,1,0:T(8,128)(2,1)} %param.11) | copy-start | bytes 2359300
  6.5 134.3 %all-gather.6.cloned.1.call-start = ((), (), s32[]{:S(2)}) async-start(), calls=%async_computation.4 | async-start | bytes 8912896 | tf_op jit(solution)/shard_map/all_gather | solution.py:30
  58.4 196.7 %all-gather.4.cloned.1.call-start = ((), (), s32[]{:S(2)}) async-start(), calls=%async_computation.3 | async-start | bytes 13369344 | tf_op jit(solution)/shard_map/all_gather | solution.py:37
  140.8 6.0 %copy-start.3 = (bf16[512,2,4096]{2,0,1:T(8,128)(2,1)S(1)}, bf16[512,2,4096]{2,0,1:T(8,128)(2,1)}, u32[]{:S(2)}) copy-start(bf16[512,2,4096]{2,0,1:T(8,128)(2,1)} %all-gather.6.cloned.1.call-done) | copy-start | bytes 25165828
  140.8 6.1 %copy-start.4 = (bf16[1,96,4096]{2,1,0:T(8,128)(2,1)S(1)}, bf16[1,96,4096]{2,1,0:T(8,128)(2,1)}, u32[]{:S(2)}) copy-start(bf16[1,96,4096]{2,1,0:T(8,128)(2,1)} %param.10) | copy-start | bytes 2359300
  268.6 54.9 %copy-start.2 = (f32[7,8]{1,0:T(8,128)S(1)}, f32[7,8]{1,0:T(8,128)}, u32[]{:S(2)}) copy-start(f32[7,8]{1,0:T(8,128)} %param.8) | copy-start | bytes 676
  268.6 55.1 %copy-start.1 = (s32[7,8]{1,0:T(8,128)S(1)}, s32[7,8]{1,0:T(8,128)}, u32[]{:S(2)}) copy-start(s32[7,8]{1,0:T(8,128)} %param.7) | copy-start | bytes 676
  317.7 16.9 %all-to-all-start.2 = ((bf16[16,32,2,256]{3,2,1,0:T(2,128)(2,1)}), bf16[16,32,2,256]{3,2,1,0:T(2,128)(2,1)S(1)}, u32[]{:S(2)}, u32[]{:S(2)}) async-start(bf16[16,32,2,256]{3,2,1,0:T(2,128)(2,1)} %copy.41), calls=%async_computation.2 | async-start | bytes 1048576 | tf_op jit(solution)/shard_map/all_to_all | solution.py:44
Sparse Core Ops, SparseCore 0:
  58.6 82.1 all-gather.5
  151.5 103.6 all-gather.3
where the time goes:
time: 344 us; the launch traced here: 343 us
  waiting for transfers between devices  197 us (57%)
  blocking collectives  92.5 us (27%)
  local copies, waits for them, and re-layouts  19.6 us (6%)
  between operations  13.5 us (4%)
  matrix products  13.4 us (4%)
  starting transfers between devices  5.81 us (2%)
    all_gather x1, waiting for transfers between devices, on_device(): lax.all_gather(hidden, 'fsdp', axis=4, tiled=True)  104 us
    all_gather x1, waiting for transfers between devices, on_device(): portion = lax.all_gather(arrived[None], 'fsdp', axis=0, tiled=True)  82.3 us
    all_to_all x1, blocking collectives, on_device(): lax.all_to_all(outgoing, 'expert', split_axis=0, concat_axis=0, tiled=True)  48.1 us
    all_to_all x1, blocking collectives, on_device(): lax.all_to_all(expert_out, 'expert', split_axis=1, concat_axis=1, tiled=T...  44.3 us
    all_gather x1, local copies, waits for them, and re-layouts, on_device(): lax.all_gather(hidden, 'fsdp', axis=4, tiled=True)  13.4 us
    all_to_all x1, waiting for transfers between devices, on_device(): lax.all_to_all(lax.all_to_all(expert_out, 'expert', split_axis=1, concat_...  10.9 us
  transfers between devices with their start and end apart: 3, of which 3 were waited for; matrix products, arithmetic and copies ran while one was open for 0% of the time, Pallas kernels for 0%

commit v1 on v0

--- a/solution.py
+++ b/solution.py
@@ -1,7 +1,20 @@
+import functools
 import jax
 import jax.numpy as jnp
 from jax import lax
 from jax.sharding import PartitionSpec as P
+
+
+def spots_wrap(array_here, axis_id, dimension_no):
+    so_far_all = []
+    for _ in range(lax.axis_size(axis_id)):
+        so_far_all.append(array_here)
+    reply = jnp.stack(so_far_all, 0)
+    b_now = lax.all_to_all(reply, axis_id, 0, 0)
+    return jnp.concatenate(b_now, dimension_no)
+
+
+ticks_apply = functools.partial(spots_wrap, axis_id="fsdp", dimension_no=4)
 
 
 def on_device(tokens, expert_ids, gate_scores, w_gate, w_up, w_down):
@@ -33,10 +46,7 @@
     up_act = jnp.einsum("knjcd,jhd->knjch", routed, w_up, preferred_element_type=jnp.float32)
     hidden = (jax.nn.silu(gate_act) * up_act).astype(jnp.bfloat16)
     summed = jnp.einsum(
-        "fnjch,jhd->fnjcd",
-        lax.all_gather(hidden, "fsdp", axis=4, tiled=True),
-        w_down,
-        preferred_element_type=jnp.float32,
+        "fnjch,jhd->fnjcd", ticks_apply(hidden), w_down, preferred_element_type=jnp.float32
     )
     expert_out = summed.astype(jnp.bfloat16).reshape(
         n_fsdp, n_expert, per_column * capacity, feature_cols

time: 344 us -> 296 us (0.86)
  waiting for transfers between devices: 197 us -> 93.3 us
  blocking collectives: 92.5 us -> 145 us
    all_gather x1 -> x0, waiting for transfers between devices: 104 us -> none  [on_device(): lax.all_gather(hidden, 'fsdp', axis=4, tiled=True)]
    all_to_all x0 -> x1, blocking collectives: none -> 53.3 us  [spots_wrap(): b_now = lax.all_to_all(reply, axis_id, 0, 0)]
    all_gather x1 -> x0, local copies, waits for them, and re-layouts: 13.4 us -> none  [on_device(): lax.all_gather(hidden, 'fsdp', axis=4, tiled=True)]
    another operation x0 -> x2, local copies, waits for them, and re-layouts: none -> 9.13 us
    reshape x0 -> x1, local copies, waits for them, and re-layouts: none -> 8.6 us  [spots_wrap(): return jnp.concatenate(b_now, dimension_no)]
  transfers between devices with their start and end apart: 3 -> 2, of which waited for: 3 -> 2; matrix products, arithmetic and copies ran while one was open for 0% -> 0% of each run, Pallas kernels for 0% -> 0%
where the time goes in v1:
time: 296 us
  blocking collectives  145 us (49%)
  waiting for transfers between devices  93.3 us (32%)
  local copies, waits for them, and re-layouts  21.9 us (7%)
  matrix products  13.5 us (5%)
  between operations  13.5 us (5%)
  starting transfers between devices  7.53 us (3%)
    all_gather x1, waiting for transfers between devices, on_device(): portion = lax.all_gather(arrived[None], 'fsdp', axis=0, tiled=True)  82.4 us
    all_to_all x1, blocking collectives, spots_wrap(): b_now = lax.all_to_all(reply, axis_id, 0, 0)  53.3 us
    all_to_all x1, blocking collectives, on_device(): lax.all_to_all(outgoing, 'expert', split_axis=0, concat_axis=0, tiled=True)  48.1 us
    all_to_all x1, blocking collectives, on_device(): lax.all_to_all(expert_out, 'expert', split_axis=1, concat_axis=1, tiled=T...  43.5 us
    all_to_all x1, waiting for transfers between devices, on_device(): lax.all_to_all(lax.all_to_all(expert_out, 'expert', split_axis=1, concat_...  10.9 us
    reshape x1, local copies, waits for them, and re-layouts, spots_wrap(): return jnp.concatenate(b_now, dimension_no)  8.6 us
    another operation x1, local copies, waits for them, and re-layouts  8.08 us
    all_to_all x1, starting transfers between devices, on_device(): lax.all_to_all(lax.all_to_all(expert_out, 'expert', split_axis=1, concat_...  7.52 us
  transfers between devices with their start and end apart: 2, of which 2 were waited for; matrix products, arithmetic and copies ran while one was open for 0% of the time, Pallas kernels for 0%

profile of v1, /device:TPU:1, one launch (start us, length us, event | category | flops | bytes accessed | tf_op | source)
XLA Modules:
  0.0 295.6 jit_solution(973012164334601140)
XLA Ops:
  6.5 0.0 copy-start
  6.5 0.0 all-gather.3.cloned.1.call-start
  6.5 0.8 convert_reduce_fusion
  7.4 1.2 convolution_convert_fusion
  8.6 0.5 copy.31
  9.2 48.1 %all_to_all.30 = bf16[32,2,4096]{2,1,0:T(2,128)(2,1)S(1)} all-to-all(bf16[32,2,4096]{2,1,0:T(2,128)(2,1)S(1)} %copy.31), channel_id=1, replica_groups=mesh['expert'=32,'fsdp'=16] {'expert'}, dimensions={0} | all-to-all | bytes 1048576 | tf_op jit(solution)/shard_map/all_to_all | solution.py:42
  57.3 1.1 copy.32
  58.4 0.0 all-gather.3.cloned.1.call-update
  58.4 82.4 %all-gather.3.cloned.1.call-done = bf16[512,2,4096]{2,0,1:T(8,128)(2,1)} async-done(((bf16[32,2,4096]{2,0,1:T(8,128)(2,1)}), bf16[512,2,4096]{2,0,1:T(8,128)(2,1)}) %all-gather.3.cloned.1.call-update) | async-done | bytes 8388624 | tf_op jit(solution)/shard_map/all_gather | solution.py:43
  140.8 0.0 copy-start.3
  140.8 0.0 copy-start.4
  140.8 6.0 %fusion.5 = f32[16,32,1,2,96]{4,1,3,0,2:T(8,128)S(1)} fusion(bf16[16,32,2,4096]{3,1,0,2:T(8,128)(2,1)} %bitcast.71, bf16[1,96,4096]{2,1,0:T(8,128)(2,1)} %param.9), kind=kOutput, calls=%fused_computation.8 | convolution fusion | flops 805306368 | bytes 9568256 | tf_op jit(solution)/shard_map/knjcd,jhd->knjch/dot_general | solution.py:45
  146.8 0.0 copy-done.3
  146.8 0.1 copy-done.4
  146.9 2.4 fusion.17
  149.3 1.1 stack.2
  150.4 53.3 %all_to_all.31 = bf16[16,16,32,1,2,96]{5,2,4,1,3,0:T(8,128)(2,1)S(1)} all-to-all(bf16[16,16,32,1,2,96]{5,2,4,1,3,0:T(8,128)(2,1)S(1)} %stack.2), channel_id=1, replica_groups=mesh['expert'=32,'fsdp'=16] {'fsdp'}, dimensions={0} | all-to-all | bytes 6291456 | tf_op jit(solution)/shard_map/all_to_all | solution.py:13
  203.7 8.6 %copy.35 = bf16[16,32,1,2,16,96]{5,4,1,3,0,2:T(8,128)(2,1)} copy(bf16[16,32,1,2,16,96]{5,1,3,0,2,4:T(8,128)(2,1)S(1)} %bitcast.68) | data formatting | bytes 6291456 | tf_op jit(solution)/shard_map/reshape | solution.py:14
  212.3 0.0 copy-start.2
  212.3 0.0 copy-start.1
  212.3 8.1 %reshape.54 = bf16[16,32,2,1536]{3,1,2,0:T(8,128)(2,1)} reshape(bf16[16,32,1,2,16,96]{5,4,1,3,0,2:T(8,128)(2,1)} %copy.35) | data formatting | bytes 6291456 | tf_op jit(solution)/shard_map/reshape.13
  220.4 0.0 copy-done
  220.4 2.9 convolution_convert_fusion.1
  223.2 0.5 copy.36
  223.8 43.5 %all_to_all.32 = bf16[16,32,2,256]{3,2,0,1:T(2,128)(2,1)S(1)} all-to-all(bf16[16,32,2,256]{3,2,0,1:T(2,128)(2,1)S(1)} %copy.36), channel_id=1, replica_groups=mesh['expert'=32,'fsdp'=16] {'expert'}, dimensions={1} | all-to-all | bytes 1048576 | tf_op jit(solution)/shard_map/all_to_all | solution.py:55
  267.2 1.3 copy.37
  268.5 7.5 %all-to-all-start.3 = ((bf16[16,32,2,256]{3,2,1,0:T(2,128)(2,1)}), bf16[16,32,2,256]{3,2,1,0:T(2,128)(2,1)S(1)}, u32[]{:S(2)}, u32[]{:S(2)}) async-start(bf16[16,32,2,256]{3,2,1,0:T(2,128)(2,1)} %copy.37), calls=%async_computation.3 | async-start | bytes 1048576 | tf_op jit(solution)/shard_map/all_to_all | solution.py:54
  276.1 0.0 copy-done.2
  276.1 0.1 reduce_sum.28
  276.2 0.1 broadcast_divide_fusion
  276.3 0.0 copy-done.1
  276.3 0.1 fusion.25
  276.4 10.9 %all-to-all-done.3 = bf16[16,32,2,256]{3,2,1,0:T(2,128)(2,1)S(1)} async-done(((bf16[16,32,2,256]{3,2,1,0:T(2,128)(2,1)}), bf16[16,32,2,256]{3,2,1,0:T(2,128)(2,1)S(1)}, u32[]{:S(2)}, u32[]{:S(2)}) %all-to-all-start.3) | async-done | bytes 524320 | tf_op jit(solution)/shard_map/all_to_all | solution.py:54
  287.2 0.3 copy.38
  287.5 0.2 reshape.56
  287.8 1.0 fusion.4
  (3 shorter events, 0.0 us)
Async XLA Ops:
  6.5 213.8 %copy-start = (bf16[1,1536,256]{2,1,0:T(8,128)(2,1)S(1)}, bf16[1,1536,256]{2,1,0:T(8,128)(2,1)}, u32[]{:S(2)}) copy-start(bf16[1,1536,256]{2,1,0:T(8,128)(2,1)} %param.11) | copy-start | bytes 2359300
  6.5 134.3 %all-gather.3.cloned.1.call-start = ((), (), s32[]{:S(2)}) async-start(), calls=%async_computation.4 | async-start | bytes 8912896 | tf_op jit(solution)/shard_map/all_gather | solution.py:43
  140.8 6.0 %copy-start.3 = (bf16[512,2,4096]{2,0,1:T(8,128)(2,1)S(1)}, bf16[512,2,4096]{2,0,1:T(8,128)(2,1)}, u32[]{:S(2)}) copy-start(bf16[512,2,4096]{2,0,1:T(8,128)(2,1)} %all-gather.3.cloned.1.call-done) | copy-start | bytes 25165828
  140.8 6.1 %copy-start.4 = (bf16[1,96,4096]{2,1,0:T(8,128)(2,1)S(1)}, bf16[1,96,4096]{2,1,0:T(8,128)(2,1)}, u32[]{:S(2)}) copy-start(bf16[1,96,4096]{2,1,0:T(8,128)(2,1)} %param.10) | copy-start | bytes 2359300
  212.3 63.8 %copy-start.2 = (f32[7,8]{1,0:T(8,128)S(1)}, f32[7,8]{1,0:T(8,128)}, u32[]{:S(2)}) copy-start(f32[7,8]{1,0:T(8,128)} %param.8) | copy-start | bytes 676
  212.3 64.0 %copy-start.1 = (s32[7,8]{1,0:T(8,128)S(1)}, s32[7,8]{1,0:T(8,128)}, u32[]{:S(2)}) copy-start(s32[7,8]{1,0:T(8,128)} %param.7) | copy-start | bytes 676
  268.5 18.7 %all-to-all-start.3 = ((bf16[16,32,2,256]{3,2,1,0:T(2,128)(2,1)}), bf16[16,32,2,256]{3,2,1,0:T(2,128)(2,1)S(1)}, u32[]{:S(2)}, u32[]{:S(2)}) async-start(bf16[16,32,2,256]{3,2,1,0:T(2,128)(2,1)} %copy.37), calls=%async_computation.3 | async-start | bytes 1048576 | tf_op jit(solution)/shard_map/all_to_all | solution.py:54
Sparse Core Ops, SparseCore 0:
  58.5 82.2 all-gather.2
